TPU v7x, 32 devices: a whole 2x2x4 slice. The times are simulated.
32 devices in a mesh: dp: 4 (over x, core), pipe: 8 (over z, y).
Axes of the slice: x: 2, y: 2, z: 4, core: 2. Of those that a mesh axis runs over, the one named last changes fastest.
Arguments:
- pre: bfloat16 [512, 49152], P('dp', 'pipe'), may hold values from -6 to 6
- grad_out: bfloat16 [512, 6144], P('dp', 'pipe'), may hold values from -6 to 6
- weight_slots: bfloat16 [8, 292, 128, 128], P('pipe', 'dp'), may hold values from -0.21875 to 0.21875
- block_rows: int32 [8, 292], P('pipe', 'dp'), may hold values from 0 to 47, as said below
- block_cols: int32 [8, 292], P('pipe', 'dp'), may hold values from 0 to 47, as said below
- block_count: int32 [8, 4], P('pipe', 'dp'), may hold values from 0 to 73, as said below
Outputs:
- pre_grad: bfloat16 [512, 49152], P('dp', 'pipe')
- weight_grad: bfloat16 [8, 292, 128, 128], P('pipe', 'dp')
Inputs may be any that keep to these rules, and one draw needn't show every extreme that they name: `block_rows`: live slots of slab p list each of its 48 rows of blocks exactly 6 times, with distinct columns; dead slots hold valid indices. `block_cols`: within a row of blocks the live columns are distinct. `block_count`: the counts of one slab sum to 288; in every slab some device holds exactly 73.
All inputs are finite; a program needn't handle non-finite values.
Results may differ from a plain program's by a relative error of at most 0.009.
Values may be sent and summed in bfloat16 or wider, within the bound.
A program may use at most 128 MiB of HBM per device.

v0:
```python
import jax
import jax.numpy as jnp
from jax import lax
from jax.sharding import PartitionSpec as P

BLOCK = 128


inv_root_two = 0.7071067811865476
inverse_square_root_tau = 0.3989422804014327


def gelu_parts(pre_wide):
    normal_cdf = 0.5 * (1.0 + jax.scipy.special.erf(pre_wide * inv_root_two))
    density = jnp.exp(-0.5 * pre_wide * pre_wide) * inverse_square_root_tau
    return (pre_wide * normal_cdf, normal_cdf + pre_wide * density)


def on_device(pre, grad_out, weight_slots, block_rows, block_cols, block_count):
    tok_rows = pre.shape[0]
    slab_rows = pre.shape[1] // BLOCK
    slot_cap = weight_slots.shape[1]
    whole_grad = lax.all_gather(grad_out, "pipe", axis=1, tiled=True)
    grad_blocks = whole_grad.reshape(tok_rows, -1, BLOCK)
    pre_wide = pre.astype(jnp.float32)
    activation, slopes = gelu_parts(pre_wide)
    activation = activation.astype(jnp.bfloat16)
    act_blocks = activation.reshape(tok_rows, slab_rows, BLOCK)
    row_range = jnp.arange(slab_rows)
    all_rows, all_cols, all_counts = (
        lax.all_gather(block_rows, "dp", axis=1, tiled=True),
        lax.all_gather(block_cols, "dp", axis=1, tiled=True),
        lax.all_gather(block_count, "dp", axis=1, tiled=True),
    )
    live_all = jnp.arange(all_rows.shape[1]) % slot_cap < jnp.repeat(all_counts[0], slot_cap)
    row_ids = all_rows[0]
    col_ids = all_cols[0]
    live_mask = live_all
    gradient_fragments = grad_blocks[:, col_ids, :]
    masked = (
        lax.all_gather(weight_slots, "dp", axis=1, tiled=True)[0]
        * live_mask.astype(jnp.bfloat16)[:, None, None]
    )
    value_portion = jnp.einsum(
        "tkd,khd->tkh", gradient_fragments, masked, preferred_element_type=jnp.float32
    )
    row_hot = (row_ids[:, None] == row_range[None, :]).astype(jnp.float32)
    hidden_grad = jnp.einsum("tkh,kr->trh", value_portion, row_hot)
    row_ids = all_rows[0]
    col_ids = all_cols[0]
    live_mask = live_all
    act_pieces = act_blocks[:, row_ids, :]
    gradient_fragments = grad_blocks[:, col_ids, :]
    grad_term = jnp.einsum(
        "tkh,tkd->khd", act_pieces, gradient_fragments, preferred_element_type=jnp.float32
    )
    own_grad = lax.psum_scatter(
        (grad_term * live_mask.astype(jnp.float32)[:, None, None]).astype(jnp.bfloat16),
        "dp",
        scatter_dimension=0,
        tiled=True,
    )
    weight_grad = own_grad[None]
    pre_grad = (hidden_grad.reshape(tok_rows, -1) * slopes).astype(jnp.bfloat16)
    return (pre_grad, weight_grad)


def solution(mesh):
    in_specs = (
        P("dp", "pipe"),
        P("dp", "pipe"),
        P("pipe", "dp", None, None),
        P("pipe", "dp"),
        P("pipe", "dp"),
        P("pipe", "dp"),
    )
    out_specs = (P("dp", "pipe"), P("pipe", "dp", None, None))
    return jax.shard_map(
        on_device, mesh=mesh, in_specs=in_specs, out_specs=out_specs, check_vma=False
    )
```

profile of v0, /device:TPU:0, one launch (start us, length us, event | category | flops | bytes accessed | tf_op | source)
XLA Modules:
  0.0 271.9 jit_solution(10886016366637159782)
XLA Ops:
  7.2 1.9 copy.18
  9.1 0.7 all-gather.3.cloned.1.call-update
  10.5 1.2 dynamic-slice
  12.4 0.7 bitcast_dynamic-update-slice_fusion.1
  13.1 0.8 bitcast_dynamic-update-slice_fusion
  13.9 0.7 bitcast_dynamic-update-slice_fusion.2
  14.6 6.4 %all-reduce.3 = (s32[292]{0:T(512)S(1)}, s32[4]{0:T(128)S(1)}, s32[292]{0:T(512)S(1)}) all-reduce(s32[292]{0:T(512)S(1)} %bitcast_dynamic-update-slice_fusion, s32[4]{0:T(128)S(1)} %bitcast_dynamic-update-slice_fusion.1, s32[292]{0:T(512)S(1)} %bitcast_dynamic-update-slice_fusion.2), channel_id=1, replica_groups=mesh['dp'=4,'pipe'=8] {'dp'}, use_global_device_ids=true, to_apply=%add.2 | all-reduce | flops 588 | bytes 4704
  21.1 0.1 reshape.94
  21.3 1.6 copy.21
  22.9 34.8 %all-gather.5.cloned.1.call-done = bf16[128,6144]{0,1:T(8,128)(2,1)} async-done(((bf16[128,768]{0,1:T(8,128)(2,1)}), bf16[128,6144]{0,1:T(8,128)(2,1)}) %all-gather.5.cloned.1.call-update) | async-done | bytes 1572880 | tf_op jit(solution)/shard_map/all_gather | solution.py:23
  57.7 1.9 copy.19
  59.6 11.1 %gather_fusion = bf16[292,128,128]{2,1,0:T(8,128)(2,1)} fusion(bf16[128,48,128]{2,0,1:T(8,128)(2,1)S(1)} %copy.19, s32[1024]{0:T(1024)S(1)} %pad_clamp_fusion.1), kind=kCustom, calls=%fused_computation | custom fusion | bytes 19137680 | tf_op jit(solution)/shard_map/gather | solution.py:39
  70.7 51.8 %all-gather.3.cloned.1.call-done = bf16[1,292,128,128]{3,2,0,1:T(8,128)(2,1)} async-done(((bf16[1,73,128,128]{3,2,0,1:T(8,128)(2,1)}), bf16[1,292,128,128]{3,2,0,1:T(8,128)(2,1)}) %all-gather.3.cloned.1.call-update) | async-done | bytes 9568272 | tf_op jit(solution)/shard_map/all_gather | solution.py:41
  122.6 12.9 %fusion.5 = bf16[128,292,128]{0,2,1:T(8,128)(2,1)} fusion(bf16[292,128,128]{2,1,0:T(8,128)(2,1)} %gather_fusion, bf16[1,292,128,128]{3,2,0,1:T(8,128)(2,1)} %all-gather.3.cloned.1.call-done, bf16[292]{0:T(512)(128)(2,1)S(1)} %convert_element_type.27), kind=kOutput, calls=%fused_computation.9 | convolution fusion | flops 1229520896 | bytes 28705352 | tf_op jit(solution)/shard_map/tkd,khd->tkh/dot_general | solution.py:44
  135.5 13.7 %copy.20 = bf16[128,292,128]{2,1,0:T(8,128)(2,1)} copy(bf16[128,292,128]{0,2,1:T(8,128)(2,1)} %fusion.5) | data formatting | bytes 19136512 | tf_op jit(solution)/shard_map/tkd,khd->tkh/transpose | solution.py:44
  149.2 7.5 %convolution_bitcast_fusion = f32[128,48,128]{2,1,0:T(8,128)} fusion(bf16[128,292,128]{2,1,0:T(8,128)(2,1)} %copy.20, s32[292]{0:T(512)S(1)} %get-tuple-element.8), kind=kOutput, calls=%fused_computation.25 | convolution fusion | flops 459290304 | bytes 12715152 | tf_op jit(solution)/shard_map/tkh,kr->trh/dot_general | solution.py:48
  156.6 2.4 copy.27
  159.1 4.0 %fusion.21 = (bf16[128,6144]{0,1:T(8,128)(2,1)}, bf16[128,6144]{0,1:T(8,128)(2,1)}) fusion(bf16[128,6144]{0,1:T(8,128)(2,1)} %copy.21, f32[128,48,128]{0,2,1:T(8,128)S(1)} %copy.27), kind=kLoop, calls=%fused_computation.24 | loop fusion | flops 10223616 | bytes 7864320 | tf_op jit(solution)/shard_map/convert_element_type | solution.py:27
  163.0 1.9 copy.23
  164.9 10.5 %gather_fusion.1 = bf16[292,128,128]{2,1,0:T(8,128)(2,1)} fusion(bf16[128,48,128]{2,0,1:T(8,128)(2,1)S(1)} %copy.23, s32[1024]{0:T(1024)S(1)} %pad_clamp_fusion), kind=kCustom, calls=%fused_computation.1 | custom fusion | bytes 19137680 | tf_op jit(solution)/shard_map/gather | solution.py:52
  175.4 11.1 %multiply_convert_fusion = bf16[292,128,128]{2,1,0:T(8,128)(2,1)} fusion(f32[292]{0:T(512)S(1)} %get-tuple-element.9, bf16[292,128,128]{2,1,0:T(8,128)(2,1)} %gather_fusion, bf16[292,128,128]{2,1,0:T(8,128)(2,1)} %gather_fusion.1), kind=kOutput, calls=%fused_computation.2 | convolution fusion | flops 1234305024 | bytes 28705936 | tf_op jit(solution)/shard_map/tkh,tkd->khd/dot_general | solution.py:54
  186.5 1.4 copy-done
  187.9 1.6 copy.25
  189.4 76.0 %reduce-scatter.2.cloned.1.call-done = bf16[73,128,128]{2,1,0:T(8,128)(2,1)} async-done(((bf16[292,128,128]{2,1,0:T(8,128)(2,1)}), bf16[73,128,128]{2,1,0:T(8,128)(2,1)}) %reduce-scatter.2.cloned.1.call-update) | async-done | bytes 2392080 | tf_op jit(solution)/shard_map/reduce_scatter | solution.py:57
  (18 shorter events, 0.3 us)
Async XLA Ops:
  7.2 14.1 %copy-start.1 = (bf16[128,6144]{1,0:T(8,128)(2,1)S(1)}, bf16[128,6144]{1,0:T(8,128)(2,1)}, u32[]{:S(2)}) copy-start(bf16[128,6144]{1,0:T(8,128)(2,1)} %param.6) | copy-start | bytes 4718596
  7.2 50.5 %all-gather.5.cloned.1.call-start = ((), (), s32[]{:S(2)}) async-start(), calls=%async_computation.2 | async-start | bytes 1769472 | tf_op jit(solution)/shard_map/all_gather | solution.py:23
  9.1 113.5 %all-gather.3.cloned.1.call-start = ((), (), s32[]{:S(2)}) async-start(), calls=%async_computation.1 | async-start | bytes 11960320 | tf_op jit(solution)/shard_map/all_gather | solution.py:41
  9.8 255.5 %reduce-scatter.2.cloned.1.call-start = ((), (), s32[]{:S(2)}) async-start(), calls=%async_computation.3 | async-start | bytes 11960320 | tf_op jit(solution)/shard_map/reduce_scatter | solution.py:57
  186.5 1.4 copy-start
Sparse Core Ops, SparseCore 0:
  10.7 46.8 all-gather.4
  59.2 63.3 all-gather.2
  186.6 78.7 reduce-scatter.1
where the time goes:
time: 273 us; the launch traced here: 272 us
  waiting for transfers between devices  163 us (60%)
  local copies, waits for them, and re-layouts  51.4 us (19%)
  matrix products  31.5 us (12%)
  between operations  15.1 us (6%)
  blocking collectives  6.44 us (2%)
  other arithmetic  4.04 us (1%)
    reduce_scatter x1, waiting for transfers between devices, on_device(): lax.psum_scatter((grad_term * live_mask.astype(jnp.float32)[:, None, None...  76 us
    all_gather x1, waiting for transfers between devices, on_device(): lax.all_gather(weight_slots, 'dp', axis=1, tiled=True)[0]  51.8 us
    all_gather x1, waiting for transfers between devices, on_device(): whole_grad = lax.all_gather(grad_out, 'pipe', axis=1, tiled=True)  34.8 us
    transpose x1, local copies, waits for them, and re-layouts, on_device(): jnp.einsum('tkd,khd->tkh', gradient_fragments, masked, preferred_element_...  13.7 us
    dot_general x1, matrix products, on_device(): jnp.einsum('tkd,khd->tkh', gradient_fragments, masked, preferred_element_...  12.9 us
    gather x1, local copies, waits for them, and re-layouts, on_device(): gradient_fragments = grad_blocks[:, col_ids, :]  11.1 us
    dot_general x1, matrix products, on_device(): jnp.einsum('tkh,tkd->khd', act_pieces, gradient_fragments, preferred_elem...  11.1 us
    gather x1, local copies, waits for them, and re-layouts, on_device(): act_pieces = act_blocks[:, row_ids, :]  10.5 us
  transfers between devices with their start and end apart: 3, of which 3 were waited for; matrix products, arithmetic and copies ran while one was open for 7% of the time, Pallas kernels for 0%

commit v1 on v0

v1 whole, which is shorter than its diff:
```python
import functools

import jax
import jax.numpy as jnp
from jax import lax
from jax.experimental import pallas as pl
from jax.experimental.pallas import tpu as pltpu
from jax.sharding import PartitionSpec as P

BLOCK = 128
UNROLL = 8
MESH = pl.DeviceIdType.MESH

inv_root_two = 0.7071067811865476
inverse_square_root_tau = 0.3989422804014327


def gelu_parts(pre_wide):
    normal_cdf = 0.5 * (1.0 + jax.scipy.special.erf(pre_wide * inv_root_two))
    density = jnp.exp(-0.5 * pre_wide * pre_wide) * inverse_square_root_tau
    return (pre_wide * normal_cdf, normal_cdf + pre_wide * density)


def plain_plan(pre, grad_out, weight_slots, block_rows, block_cols, block_count):
    tok_rows = pre.shape[0]
    slab_rows = pre.shape[1] // BLOCK
    slot_cap = weight_slots.shape[1]
    whole_grad = lax.all_gather(grad_out, "pipe", axis=1, tiled=True)
    grad_blocks = whole_grad.reshape(tok_rows, -1, BLOCK)
    activation, slopes = gelu_parts(pre.astype(jnp.float32))
    activation = activation.astype(jnp.bfloat16)
    act_blocks = activation.reshape(tok_rows, slab_rows, BLOCK)
    row_range = jnp.arange(slab_rows)
    row_ids = lax.all_gather(block_rows, "dp", axis=1, tiled=True)[0]
    col_ids = lax.all_gather(block_cols, "dp", axis=1, tiled=True)[0]
    counts = lax.all_gather(block_count, "dp", axis=1, tiled=True)
    live = jnp.arange(row_ids.shape[0]) % slot_cap < jnp.repeat(counts[0], slot_cap)
    fragments = grad_blocks[:, col_ids, :]
    masked = (
        lax.all_gather(weight_slots, "dp", axis=1, tiled=True)[0]
        * live.astype(jnp.bfloat16)[:, None, None]
    )
    value_portion = jnp.einsum(
        "tkd,khd->tkh", fragments, masked, preferred_element_type=jnp.float32
    )
    row_hot = (row_ids[:, None] == row_range[None, :]).astype(jnp.float32)
    hidden_grad = jnp.einsum("tkh,kr->trh", value_portion, row_hot)
    grad_term = jnp.einsum(
        "tkh,tkd->khd", act_blocks[:, row_ids, :], fragments, preferred_element_type=jnp.float32
    )
    own_grad = lax.psum_scatter(
        (grad_term * live.astype(jnp.float32)[:, None, None]).astype(jnp.bfloat16),
        "dp",
        scatter_dimension=0,
        tiled=True,
    )
    pre_grad = (hidden_grad.reshape(tok_rows, -1) * slopes).astype(jnp.bfloat16)
    return (pre_grad, own_grad[None])


def gather_kernel(depth, cols, grad, pre, weights, meta, g, pre_x, w_core, meta_core,
                  local_sem, chunk_recv, z_send, y_send, x_send, flat_send, flat_recv):
    dp, pipe = lax.axis_index("dp"), lax.axis_index("pipe")
    x, core = dp // 2, dp % 2
    z, y = pipe // 2, pipe % 2
    x_to = ((1 - x) * 2 + core, pipe)
    core_to = (x * 2 + 1 - core, pipe)
    y_to = (dp, z * 2 + 1 - y)
    up_to, down_to = (dp, pipe + 2), (dp, pipe - 2)
    has_up, has_down = z < depth - 1, z > 0

    def greet(who):
        pl.semaphore_signal(barrier, inc=1, device_id=who, device_id_type=MESH)

    def chunk(zz, yy, xx):
        return g.at[pl.ds((zz * 2 + yy) * cols, cols), xx]

    def send(src, dst, send_sem, recv_sem, who):
        return pltpu.make_async_remote_copy(
            src_ref=src, dst_ref=dst, send_sem=send_sem, recv_sem=recv_sem,
            device_id=who, device_id_type=MESH)

    barrier = pltpu.get_barrier_semaphore()
    locals_ = [
        pltpu.make_async_copy(
            grad.at[:, pl.ds(c * BLOCK, BLOCK)], g.at[pipe * cols + c, x], local_sem.at[c])
        for c in range(cols)
    ]
    for copy in locals_:
        copy.start()
    for who in (x_to, core_to, y_to):
        greet(who)

    @pl.when(has_up)
    def _():
        greet(up_to)

    @pl.when(has_down)
    def _():
        greet(down_to)

    pl.semaphore_wait(barrier, 3 + has_up.astype(jnp.int32) + has_down.astype(jnp.int32))
    for copy in locals_:
        copy.wait()
    mine = chunk(z, y, x)
    shard_x = send(mine, mine, x_send.at[0], chunk_recv.at[pipe, x], x_to)
    shard_x.start()
    flat = [
        send(meta, meta_core, flat_send.at[0], flat_recv.at[0], core_to),
        send(weights, w_core, flat_send.at[1], flat_recv.at[1], core_to),
        send(pre, pre_x, flat_send.at[2], flat_recv.at[2], x_to),
    ]
    for copy in flat:
        copy.start()

    def spread(zz, xx, xi, act):
        spot, sem = chunk(zz, y, xx), chunk_recv.at[zz * 2 + y, xx]
        act(send(spot, spot, y_send.at[zz, xx], sem, y_to))

        @pl.when(jnp.logical_and(zz <= z, has_up))
        def _():
            act(send(spot, spot, z_send.at[0, zz, xx], sem, up_to))

        @pl.when(jnp.logical_and(zz >= z, has_down))
        def _():
            act(send(spot, spot, z_send.at[1, zz, xx], sem, down_to))

    def arrived(zz, yy, xx):
        spot, sem = chunk(zz, yy, xx), chunk_recv.at[zz * 2 + yy, xx]
        send(spot, spot, y_send.at[zz, xx], sem, y_to).wait_recv()

    spread(z, x, 0, lambda copy: copy.start())
    arrived(z, y, 1 - x)
    spread(z, 1 - x, 1, lambda copy: copy.start())
    for far in range(1, depth):
        for xi, xx in enumerate((x, 1 - x)):
            for zz, there in ((z - far, z >= far), (z + far, z + far < depth)):
                @pl.when(there)
                def _(zz=zz, xx=xx, xi=xi):
                    arrived(zz, y, xx)
                    spread(zz, xx, xi, lambda copy: copy.start())

    for zz in range(depth):
        for xx in (x, 1 - x):
            arrived(zz, 1 - y, xx)
    for zz in range(depth):
        for xi, xx in enumerate((x, 1 - x)):
            spread(zz, xx, xi, lambda copy: copy.wait_send())
    shard_x.wait_send()
    for copy in flat:
        copy.wait()


def gather(depth, grad, pre, weights, meta):
    cols = grad.shape[1] // BLOCK
    blocks = cols * depth * 2
    any_spec = pl.BlockSpec(memory_space=pl.ANY)
    dma = pltpu.SemaphoreType.DMA
    return pl.pallas_call(
        functools.partial(gather_kernel, depth, cols),
        out_shape=(
            jax.ShapeDtypeStruct((blocks, 2, grad.shape[0], BLOCK), grad.dtype),
            jax.ShapeDtypeStruct(pre.shape, pre.dtype),
            jax.ShapeDtypeStruct(weights.shape, weights.dtype),
            jax.ShapeDtypeStruct(meta.shape, meta.dtype),
        ),
        in_specs=[any_spec] * 4,
        out_specs=(any_spec,) * 4,
        scratch_shapes=[
            dma((cols,)), dma((depth * 2, 2)), dma((2, depth, 2)), dma((depth, 2)),
            dma((1,)), dma((3,)), dma((3,)),
        ],
        compiler_params=pltpu.CompilerParams(collective_id=0, has_side_effects=True),
    )(grad, pre, weights, meta)


def hidden_kernel(cap, group, meta_a, meta_b, w_a, w_b, g, out, acc):
    rows = acc.shape[0] - 1
    acc[...] = jnp.zeros_like(acc)
    for meta, w in ((meta_a, w_a), (meta_b, w_b)):
        count = meta[2 * cap]

        def step(i, carry, meta=meta, w=w, count=count):
            terms = []
            for u in range(UNROLL):
                slot = i * UNROLL + u
                safe = jnp.minimum(slot, cap - 1)
                row = jnp.where(slot < count, meta[safe], rows)
                terms.append((row, lax.dot_general(
                    g[meta[cap + safe], 0], w[safe], (((1,), (1,)), ((), ())),
                    preferred_element_type=jnp.float32)))
            for row, term in terms:
                acc[row] += term
            return carry

        lax.fori_loop(0, pl.cdiv(cap, UNROLL), step, 0)
    for row in range(rows):
        out[:, row * BLOCK:(row + 1) * BLOCK] = acc[row].astype(out.dtype)


def hidden(group, meta_a, meta_b, w_a, w_b, g, rows, dtype):
    cap, tokens = w_a.shape[0], g.shape[2]
    whole = lambda shape: pl.BlockSpec(shape, lambda i, *s: (0,) * len(shape))
    return pl.pallas_call(
        functools.partial(hidden_kernel, cap),
        out_shape=jax.ShapeDtypeStruct((tokens, rows * BLOCK), dtype),
        grid_spec=pltpu.PrefetchScalarGridSpec(
            num_scalar_prefetch=3,
            grid=(1,),
            in_specs=[
                whole(w_a.shape),
                whole(w_b.shape),
                pl.BlockSpec((g.shape[0], 1, tokens, BLOCK), lambda i, group, *s: (0, group[0], 0, 0)),
            ],
            out_specs=whole((tokens, rows * BLOCK)),
            scratch_shapes=[pltpu.VMEM((rows + 1, tokens, BLOCK), jnp.float32)],
        ),
        compiler_params=pltpu.CompilerParams(vmem_limit_bytes=48 << 20),
        cost_estimate=pl.CostEstimate(
            flops=4 * cap * tokens * BLOCK * BLOCK, bytes_accessed=10 << 20, transcendentals=0),
    )(group, meta_a, meta_b, w_a, w_b, g)


def weight_kernel(cap, group, meta_a, meta_b, pre, pre_x, g, out_a, out_b, slopes, act):
    rows, tokens = act.shape[0], pre.shape[0]
    mine = pl.multiple_of(group[0] * tokens, tokens)
    other = pl.multiple_of((1 - group[0]) * tokens, tokens)

    def gelu(row, carry):
        lanes = pl.ds(pl.multiple_of(row * BLOCK, BLOCK), BLOCK)
        value, slope = gelu_parts(pre[:, lanes].astype(jnp.float32))
        slopes[:, lanes] = slope
        act[row, :, pl.ds(mine, tokens)] = value.astype(jnp.bfloat16).T
        value, _ = gelu_parts(pre_x[:, lanes].astype(jnp.float32))
        act[row, :, pl.ds(other, tokens)] = value.astype(jnp.bfloat16).T
        return carry

    lax.fori_loop(0, rows, gelu, 0)
    for meta, out in ((meta_b, out_b), (meta_a, out_a)):
        count = meta[2 * cap]

        def step(i, carry, meta=meta, out=out, count=count):
            for u in range(UNROLL):
                safe = jnp.minimum(i * UNROLL + u, cap - 1)
                piece = g[meta[cap + safe]].reshape(2 * tokens, BLOCK)
                term = jnp.dot(act[meta[safe]], piece, preferred_element_type=jnp.float32)
                out[safe] = jnp.where(safe < count, term, 0.0).astype(out.dtype)
            return carry

        lax.fori_loop(0, pl.cdiv(cap, UNROLL), step, 0)


def weight_terms(group, meta_a, meta_b, pre, pre_x, g, cap):
    tokens, rows = pre.shape[0], pre.shape[1] // BLOCK
    whole = lambda shape: pl.BlockSpec(shape, lambda i, *s: (0,) * len(shape))
    slots = (cap, BLOCK, BLOCK)
    return pl.pallas_call(
        functools.partial(weight_kernel, cap),
        out_shape=(
            jax.ShapeDtypeStruct(slots, jnp.bfloat16),
            jax.ShapeDtypeStruct(slots, jnp.bfloat16),
            jax.ShapeDtypeStruct(pre.shape, jnp.float32),
        ),
        grid_spec=pltpu.PrefetchScalarGridSpec(
            num_scalar_prefetch=3,
            grid=(1,),
            in_specs=[whole(pre.shape), whole(pre_x.shape), whole(g.shape)],
            out_specs=(whole(slots), whole(slots), whole(pre.shape)),
            scratch_shapes=[pltpu.VMEM((rows, BLOCK, 2 * tokens), jnp.bfloat16)],
        ),
        compiler_params=pltpu.CompilerParams(vmem_limit_bytes=48 << 20),
        cost_estimate=pl.CostEstimate(
            flops=8 * cap * tokens * BLOCK * BLOCK, bytes_accessed=16 << 20, transcendentals=0),
    )(group, meta_a, meta_b, pre, pre_x, g)


def pair_plan(depth, pre, grad_out, weight_slots, block_rows, block_cols, block_count):
    rows, cap = pre.shape[1] // BLOCK, weight_slots.shape[1]
    listed = jnp.concatenate([block_rows[0], block_cols[0], block_count[0]])
    meta = jnp.pad(listed, (0, -listed.shape[0] % 1024)).reshape(-1, BLOCK)
    g, pre_x, w_core, meta_core = gather(depth, grad_out, pre, weight_slots[0], meta)
    meta_a, meta_b = meta.reshape(-1), meta_core.reshape(-1)
    group = (lax.axis_index("dp") // 2).astype(jnp.int32).reshape(1)
    far = hidden(1 - group, meta_a, meta_b, weight_slots[0], w_core, g, rows, jnp.bfloat16)
    from_x = lax.ppermute(far, "dp", [(i, (i + 2) % 4) for i in range(4)])
    term_a, term_b, slopes = weight_terms(group, meta_a, meta_b, pre, pre_x, g, cap)
    from_core = lax.ppermute(term_b, "dp", [(i, i ^ 1) for i in range(4)])
    near = hidden(group, meta_a, meta_b, weight_slots[0], w_core, g, rows, jnp.float32)
    weight_grad = (term_a.astype(jnp.float32) + from_core.astype(jnp.float32)).astype(jnp.bfloat16)
    pre_grad = ((near + from_x.astype(jnp.float32)) * slopes).astype(jnp.bfloat16)
    return (pre_grad, weight_grad[None])


def solution(mesh):
    in_specs = (
        P("dp", "pipe"),
        P("dp", "pipe"),
        P("pipe", "dp", None, None),
        P("pipe", "dp"),
        P("pipe", "dp"),
        P("pipe", "dp"),
    )
    out_specs = (P("dp", "pipe"), P("pipe", "dp", None, None))
    paired = mesh.shape["dp"] == 4 and mesh.shape["pipe"] == 8
    plan = functools.partial(pair_plan, mesh.shape["pipe"] // 2) if paired else plain_plan
    return jax.shard_map(
        plan, mesh=mesh, in_specs=in_specs, out_specs=out_specs, check_vma=False
    )
```

time: 273 us -> 107 us (0.39)
  waiting for transfers between devices: 163 us -> 8.84 us
  Pallas kernels: 0 us -> 86 us
  local copies, waits for them, and re-layouts: 51.4 us -> 1.28 us
  matrix products: 31.5 us -> 0 us
  between operations: 15.1 us -> 1.52 us
  blocking collectives: 6.44 us -> 0 us
  other arithmetic: 4.04 us -> 9.24 us
    all_gather x2 -> x0, waiting for transfers between devices: 86.6 us -> none  [the longest x1 51.8 us: on_device(): lax.all_gather(weight_slots, 'dp', axis=1, tiled=True)[0]]
    pallas_call x0 -> x4, Pallas kernels: none -> 86 us  [the longest x1 49.4 us: gather(): pl.pallas_call(functools.partial(gather_kernel, depth, cols), out_shape=(...]
    reduce_scatter x1 -> x0, waiting for transfers between devices: 76 us -> none  [on_device(): lax.psum_scatter((grad_term * live_mask.astype(jnp.float32)[:, None, None...]
    dot_general x3 -> x0, matrix products: 31.5 us -> none  [the longest x1 12.9 us: on_device(): jnp.einsum('tkd,khd->tkh', gradient_fragments, masked, preferred_element_...]
    gather x2 -> x0, local copies, waits for them, and re-layouts: 21.6 us -> none  [the longest x1 11.1 us: on_device(): gradient_fragments = grad_blocks[:, col_ids, :]]
    transpose x1 -> x0, local copies, waits for them, and re-layouts: 13.7 us -> none  [on_device(): jnp.einsum('tkd,khd->tkh', gradient_fragments, masked, preferred_element_...]
    unnamed x14 -> x12, local copies, waits for them, and re-layouts: 9.78 us -> 0.69 us
    ppermute x0 -> x2, waiting for transfers between devices: none -> 8.84 us  [the longest x1 8.84 us: pair_plan(): from_x = lax.ppermute(far, 'dp', [(i, (i + 2) % 4) for i in range(4)])]
  transfers between devices with their start and end apart: 3 -> 2, of which waited for: 3 -> 1; matrix products, arithmetic and copies ran while one was open for 7% -> 4% of each run, Pallas kernels for 0% -> 25%
where the time goes in v1:
time: 107 us
  Pallas kernels  86 us (80%)
  other arithmetic  9.24 us (9%)
  waiting for transfers between devices  8.84 us (8%)
  between operations  1.52 us (1%)
  local copies, waits for them, and re-layouts  1.28 us (1%)
    pallas_call x1, Pallas kernels, gather(): pl.pallas_call(functools.partial(gather_kernel, depth, cols), out_shape=(...  49.4 us
    pallas_call x2, Pallas kernels, hidden(): pl.pallas_call(functools.partial(hidden_kernel, cap), out_shape=jax.Shape...  20.7 us
    pallas_call x1, Pallas kernels, weight_terms(): pl.pallas_call(functools.partial(weight_kernel, cap), out_shape=(jax.Shap...  15.9 us
    ppermute x1, waiting for transfers between devices, pair_plan(): from_x = lax.ppermute(far, 'dp', [(i, (i + 2) % 4) for i in range(4)])  8.84 us
    broadcast_in_dim x1, other arithmetic, pair_plan(): return (pre_grad, weight_grad[None])  4.38 us
    convert_element_type x1, other arithmetic, pair_plan(): ((near + from_x.astype(jnp.float32)) * slopes).astype(jnp.bfloat16)  4.11 us
  transfers between devices with their start and end apart: 2, of which 1 were waited for; matrix products, arithmetic and copies ran while one was open for 4% of the time, Pallas kernels for 25%

profile of v1, /device:TPU:0, one launch (start us, length us, event | category | flops | bytes accessed | tf_op | source)
XLA Modules:
  0.0 107.0 jit_solution(17900273747127075894)
XLA Ops:
  0.6 0.0 copy-start
  1.4 0.7 pad_add_fusion
  2.2 0.6 pad_bitcast_fusion
  2.8 49.4 %shard_map.77 = (bf16[48,2,128,128]{3,2,1,0:T(8,128)(2,1)}, bf16[128,6144]{1,0:T(8,128)(2,1)}, bf16[73,128,128]{2,1,0:T(8,128)(2,1)}, s32[8,128]{1,0:T(8,128)}) custom-call(bf16[128,768]{1,0:T(8,128)(2,1)} %grad.1, bf16[128,6144]{1,0:T(8,128)(2,1)} %pre.3, bf16[73,128,128]{2,1,0:T(8,128)(2,1)} %bitcast.11, s32[8,128]{1,0:T(8,128)} %get-tuple-element.16.meta), custom_call_target="tpu_custom_call" | custom-call | tf_op jit(solution)/shard_map/pallas_call | solution.py:159
  52.2 0.0 copy-done
  52.2 0.0 copy-start.4
  52.2 0.7 copy-done.4
  52.9 0.0 copy-start.2
  52.9 0.0 copy-start.3
  52.9 9.9 %shard_map.79 = bf16[128,6144]{1,0:T(8,128)(2,1)S(1)} custom-call(s32[1]{0:T(128)S(6)} %sub.8.group, s32[1024]{0:T(1024)S(1)} %get-tuple-element.17.meta_a, s32[1024]{0:T(1024)S(1)} %bitcast.14, bf16[73,128,128]{2,1,0:T(8,128)(2,1)S(1)} %bitcast.12, bf16[73,128,128]{2,1,0:T(8,128)(2,1)} %get-tuple-element.10.w_b, bf16[48,2,128,128]{3,2,1,0:T(8,128)(2,1)} %get-tuple-element.11.g), custom_call_target="tpu_custom_call" | custom-call | flops 612368384 | bytes 10485760 | tf_op jit(solution)/shard_map/pallas_call | solution.py:204
  62.8 0.1 collective-permute-start
  62.9 0.0 copy-done.2
  62.9 0.0 copy-done.3
  62.9 0.0 copy-start.1
  62.9 15.9 %shard_map.80 = (bf16[73,128,128]{2,1,0:T(8,128)(2,1)S(1)}, bf16[73,128,128]{2,1,0:T(8,128)(2,1)}, f32[128,6144]{1,0:T(8,128)}) custom-call(s32[1]{0:T(128)} %bitcast.group, s32[1024]{0:T(1024)S(1)} %get-tuple-element.17.meta_a, s32[1024]{0:T(1024)S(1)} %bitcast.15, bf16[128,6144]{1,0:T(8,128)(2,1)S(1)} %copy-done.2, bf16[128,6144]{1,0:T(8,128)(2,1)S(1)} %copy-done.3, ...), custom_call_target="tpu_custom_call" | custom-call | flops 1224736768 | bytes 16777216 | tf_op jit(solution)/shard_map/pallas_call | solution.py:257
  78.8 0.0 copy-start.5
  78.8 0.0 collective-permute-start.1
  78.8 0.0 copy-done.1
  78.8 10.9 %shard_map.78 = f32[128,6144]{1,0:T(8,128)} custom-call(s32[1]{0:T(128)} %bitcast.group, s32[1024]{0:T(1024)S(1)} %get-tuple-element.17.meta_a, s32[1024]{0:T(1024)S(1)} %bitcast.16, bf16[73,128,128]{2,1,0:T(8,128)(2,1)S(1)} %bitcast.13, bf16[73,128,128]{2,1,0:T(8,128)(2,1)S(1)} %copy-done.1, bf16[48,2,128,128]{3,2,1,0:T(8,128)(2,1)} %get-tuple-element.11.g), custom_call_target="tpu_custom_call" | custom-call | flops 612368384 | bytes 10485760 | tf_op jit(solution)/shard_map/pallas_call | solution.py:204
  89.7 8.8 %collective-permute-done = bf16[128,6144]{1,0:T(8,128)(2,1)} collective-permute-done((bf16[128,6144]{1,0:T(8,128)(2,1)S(1)}, bf16[128,6144]{1,0:T(8,128)(2,1)}, u32[]{:S(2)}, u32[]{:S(2)}) %collective-permute-start) | collective-permute-done | bytes 1572896 | tf_op jit(solution)/shard_map/ppermute | solution.py:285
  98.5 0.0 copy-done.5
  98.5 4.1 %multiply_convert_fusion = bf16[128,6144]{1,0:T(8,128)(2,1)} fusion(f32[128,6144]{1,0:T(8,128)S(1)} %copy-done.5, f32[128,6144]{1,0:T(8,128)} %shard_map.78, bf16[128,6144]{1,0:T(8,128)(2,1)} %collective-permute-done), kind=kLoop, calls=%fused_computation.1 | loop fusion | flops 3145728 | bytes 9437184 | tf_op jit(solution)/shard_map/convert_element_type | solution.py:290
  102.6 0.0 collective-permute-done.1
  102.6 4.4 %fusion = bf16[1,73,128,128]{3,2,1,0:T(8,128)(2,1)} fusion(bf16[73,128,128]{2,1,0:T(8,128)(2,1)} %collective-permute-done.1, bf16[73,128,128]{2,1,0:T(8,128)(2,1)S(1)} %get-tuple-element.14), kind=kLoop, calls=%fused_computation.2 | loop fusion | flops 4784128 | bytes 7176192 | tf_op jit(solution)/shard_map/broadcast_in_dim | solution.py:291
Async XLA Ops:
  0.6 51.6 %copy-start = (bf16[1,73,128,128]{3,2,1,0:T(8,128)(2,1)S(1)}, bf16[1,73,128,128]{3,2,1,0:T(8,128)(2,1)}, u32[]{:S(2)}) copy-start(bf16[1,73,128,128]{3,2,1,0:T(8,128)(2,1)} %param.8) | copy-start | bytes 7176196
  52.2 0.7 copy-start.4
  52.9 10.0 %copy-start.2 = (bf16[128,6144]{1,0:T(8,128)(2,1)S(1)}, bf16[128,6144]{1,0:T(8,128)(2,1)}, u32[]{:S(2)}) copy-start(bf16[128,6144]{1,0:T(8,128)(2,1)} %pre.3) | copy-start | bytes 4718596
  52.9 10.0 %copy-start.3 = (bf16[128,6144]{1,0:T(8,128)(2,1)S(1)}, bf16[128,6144]{1,0:T(8,128)(2,1)}, u32[]{:S(2)}) copy-start(bf16[128,6144]{1,0:T(8,128)(2,1)} %get-tuple-element.12.pre_x) | copy-start | bytes 4718596
  62.8 35.7 %collective-permute-start = (bf16[128,6144]{1,0:T(8,128)(2,1)S(1)}, bf16[128,6144]{1,0:T(8,128)(2,1)}, u32[]{:S(2)}, u32[]{:S(2)}) collective-permute-start(bf16[128,6144]{1,0:T(8,128)(2,1)S(1)} %shard_map.79), channel_id=1, source_target_pairs={{0,16},{8,24},{16,0},{24,8},{1,17},{9,25},{17,1},{25,9},{2,18},{10... | collective-permute-start | bytes 4718600 | tf_op jit(solution)/shard_map/ppermute | solution.py:285
  62.9 15.9 %copy-start.1 = (bf16[73,128,128]{2,1,0:T(8,128)(2,1)S(1)}, bf16[73,128,128]{2,1,0:T(8,128)(2,1)}, u32[]{:S(2)}) copy-start(bf16[73,128,128]{2,1,0:T(8,128)(2,1)} %get-tuple-element.10.w_b) | copy-start | bytes 7176196
  78.8 19.7 %copy-start.5 = (f32[128,6144]{1,0:T(8,128)S(1)}, f32[128,6144]{1,0:T(8,128)}, u32[]{:S(2)}) copy-start(f32[128,6144]{1,0:T(8,128)} %get-tuple-element.13) | copy-start | bytes 9437188
  78.8 23.8 %collective-permute-start.1 = (bf16[73,128,128]{2,1,0:T(8,128)(2,1)}, bf16[73,128,128]{2,1,0:T(8,128)(2,1)}, u32[]{:S(2)}, u32[]{:S(2)}) collective-permute-start(bf16[73,128,128]{2,1,0:T(8,128)(2,1)} %get-tuple-element.15), channel_id=1, source_target_pairs={{0,8},{8,0},{16,24},{24,16},{1,9},{9,1},{17,25},{25,17},{2,10},{10... | collective-permute-start | bytes 7176200 | tf_op jit(solution)/shard_map/ppermute | solution.py:287
